TPU v7x, 128 devices: a whole 4x4x4 slice. The times are simulated.
128 devices in a mesh: dp: 4 (over x), ctx: 32 (over z, y, core).
Axes of the slice: x: 4, y: 4, z: 4, core: 2. Of those that a mesh axis runs over, the one named last changes fastest.
Arguments:
- queries: bfloat16 [4, 8192, 2048], P('dp', 'ctx'), may hold values from -6 to 6
- keys: bfloat16 [4, 8192, 2048], P('dp', 'ctx'), may hold values from -6 to 6
- values: bfloat16 [4, 8192, 2048], P('dp', 'ctx'), may hold values from -6 to 6
- gain: float32 [2048], replicated, may hold values from 0.1 to 1.9
- out_weight: bfloat16 [2048, 4096], P('dp'), may hold values from -0.125 to 0.125
- grad_out: bfloat16 [4, 8192, 4096], P('dp', 'ctx'), may hold values from -6 to 6
Outputs:
- layer_out: bfloat16 [4, 8192, 4096], P('dp', 'ctx')
- grad_queries: bfloat16 [4, 8192, 2048], P('dp', 'ctx')
- grad_keys: bfloat16 [4, 8192, 2048], P('dp', 'ctx')
- grad_values: bfloat16 [4, 8192, 2048], P('dp', 'ctx')
- grad_weight: float32 [2048, 4096], P(('dp', 'ctx'))
All inputs are finite; a program needn't handle non-finite values.
Results may differ from a plain program's by a relative error of at most 0.015.
Values may be sent and summed in bfloat16 or wider, within the bound.
No kernel may reach another device: no remote copies, remote signals or barrier semaphores. Data moves between devices by JAX's collectives and lax.ppermute only.
A program may use at most 192 MiB of HBM per device.

v0:
```python
import math
import jax
import jax.numpy as jnp
from jax import lax
from jax.sharding import PartitionSpec as P

HD = 128
EPSILON = 1e-06
HIGHEST = lax.Precision.HIGHEST


def prefix(part, axis, combine, identity, reverse):
    count = lax.axis_size(axis)
    place = lax.axis_index(axis)
    ahead = count - 1 - place if reverse else place
    gathered = lax.all_gather(part, axis)
    state = jnp.zeros_like(part) + jnp.asarray(identity, part.dtype)

    def one(turn, state):
        source = count - 1 - turn if reverse else turn
        return combine(state, lax.dynamic_index_in_dim(gathered, source, 0, False))

    return lax.fori_loop(0, ahead, one, state)


def add_terms(earlier, later_part):
    return earlier + later_part


def shards(queries, keys, values, gain, out_weight, grad_out):
    tok_rows = queries.shape[1]
    feat_width = queries.shape[2]
    head_count = feat_width // HD
    model_width = grad_out.shape[2]
    query_rows = queries.reshape(tok_rows, head_count, HD)
    key_rows = keys.reshape(tok_rows, head_count, HD)
    value_rows = values.reshape(tok_rows, head_count, HD)
    causal = lax.broadcasted_iota(jnp.int32, (tok_rows, tok_rows), 0) >= lax.broadcasted_iota(
        jnp.int32, (tok_rows, tok_rows), 1
    )
    scores = jnp.einsum("thd,shd->hts", query_rows, key_rows, preferred_element_type=jnp.float32)
    weights = jnp.where(causal, scores, 0.0).astype(jnp.bfloat16)
    local_out = jnp.einsum("hts,shd->thd", weights, value_rows, preferred_element_type=jnp.float32)
    local_state = jnp.einsum(
        "shd,she->hde", key_rows, value_rows, preferred_element_type=jnp.float32
    )
    carried = prefix(local_state, "ctx", add_terms, jnp.zeros_like(local_state), False)
    state_out = jnp.einsum(
        "thd,hde->the", query_rows.astype(jnp.float32), carried, precision=HIGHEST
    )
    attended = local_out + state_out
    inv_rms = lax.rsqrt(jnp.mean(attended * attended, axis=-1, keepdims=True) + EPSILON)
    unit_out = attended * inv_rms
    gain_heads = gain.reshape(head_count, HD)
    normed = (unit_out * gain_heads).astype(jnp.bfloat16).reshape(tok_rows, feat_width)
    grad_rows = grad_out.reshape(tok_rows, model_width)
    full_weight = lax.all_gather(out_weight, "dp", axis=0, tiled=True)
    layer_rows = jnp.dot(normed, full_weight, preferred_element_type=jnp.float32)
    layer_out = layer_rows.astype(jnp.bfloat16).reshape(1, tok_rows, model_width)
    shared_cols = lax.all_to_all(normed, "dp", split_axis=1, concat_axis=0, tiled=True)
    grad_normed = lax.dot_general(
        grad_rows, full_weight, (((1,), (1,)), ((), ())), preferred_element_type=jnp.float32
    )
    weight_term = lax.dot_general(
        shared_cols,
        lax.all_gather(grad_rows, "dp", axis=0, tiled=True),
        (((0,), (0,)), ((), ())),
        preferred_element_type=jnp.float32,
    )
    token_count = lax.axis_size("dp") * lax.axis_size("ctx") * tok_rows
    grad_weight = lax.psum_scatter(
        weight_term.astype(jnp.bfloat16), "ctx", scatter_dimension=0, tiled=True
    ).astype(jnp.float32) * (1.0 / math.sqrt(token_count))
    grad_unit = grad_normed.reshape(tok_rows, head_count, HD) * gain_heads
    grad_attn = inv_rms * (
        grad_unit - unit_out * jnp.mean(grad_unit * unit_out, axis=-1, keepdims=True)
    )
    grad_attn = grad_attn.astype(jnp.bfloat16)
    grad_scores = jnp.einsum(
        "the,she->hts", grad_attn, value_rows, preferred_element_type=jnp.float32
    )
    grad_scores = jnp.where(causal, grad_scores, 0.0).astype(jnp.bfloat16)
    local_grad = jnp.einsum(
        "thd,the->hde", query_rows, grad_attn, preferred_element_type=jnp.float32
    )
    later = prefix(local_grad, "ctx", add_terms, jnp.zeros_like(local_grad), True)
    grad_query = jnp.einsum(
        "hts,shd->thd", grad_scores, key_rows, preferred_element_type=jnp.float32
    )
    grad_query = grad_query + jnp.einsum(
        "the,hde->thd", grad_attn.astype(jnp.float32), carried, precision=HIGHEST
    )
    grad_key = jnp.einsum(
        "hts,thd->shd", grad_scores, query_rows, preferred_element_type=jnp.float32
    )
    grad_key = grad_key + jnp.einsum(
        "she,hde->shd", value_rows.astype(jnp.float32), later, precision=HIGHEST
    )
    grad_value = jnp.einsum("hts,the->she", weights, grad_attn, preferred_element_type=jnp.float32)
    grad_value = grad_value + jnp.einsum(
        "shd,hde->she", key_rows.astype(jnp.float32), later, precision=HIGHEST
    )
    out_shape = (1, tok_rows, feat_width)
    return (
        layer_out,
        grad_query.astype(jnp.bfloat16).reshape(out_shape),
        grad_key.astype(jnp.bfloat16).reshape(out_shape),
        grad_value.astype(jnp.bfloat16).reshape(out_shape),
        grad_weight,
    )


def solution(mesh):
    in_specs = (
        P("dp", "ctx", None),
        P("dp", "ctx", None),
        P("dp", "ctx", None),
        P(),
        P("dp", None),
        P("dp", "ctx", None),
    )
    out_specs = (
        P("dp", "ctx", None),
        P("dp", "ctx", None),
        P("dp", "ctx", None),
        P("dp", "ctx", None),
        P(("dp", "ctx"), None),
    )
    return jax.shard_map(shards, mesh=mesh, in_specs=in_specs, out_specs=out_specs, check_vma=False)
```

profile of v0, /device:TPU:0, one launch (start us, length us, event | category | flops | bytes accessed | tf_op | source)
XLA Modules:
  0.0 650.7 jit_solution(872384761315528733)
XLA Ops:
  7.2 1.5 copy.78
  16.6 2.2 fusion.12
  18.7 109.2 %all-gather.10.cloned.1.call-done = f32[512,128,128]{2,1,0:T(8,128)} async-done(((f32[16,128,128]{2,1,0:T(8,128)}), f32[512,128,128]{2,1,0:T(8,128)}) %all-gather.10.cloned.1.call-update) | async-done | bytes 33554448 | tf_op jit(solution)/shard_map/all_gather | solution.py:16
  128.1 4.1 multiply_reduce_fusion.1
  132.2 150.6 %all-gather.8.cloned.1.call-done = bf16[2048,4096]{1,0:T(8,128)(2,1)} async-done(((bf16[512,4096]{1,0:T(8,128)(2,1)}), bf16[2048,4096]{1,0:T(8,128)(2,1)}) %all-gather.8.cloned.1.call-update) | async-done | bytes 16777232 | tf_op jit(solution)/shard_map/all_gather | solution.py:57
  282.8 12.6 %multiply_reduce_fusion = (f32[256,16]{0,1:T(8,128)S(1)}, f32[256,16,128]{0,2,1:T(8,128)S(1)}) fusion(f32[256,16,128]{0,2,1:T(8,128)} %get-tuple-element.128, f32[16,128]{1,0:T(8,128)S(1)} %bitcast.102, f32[256,16]{0,1:T(8,128)S(1)} %add_rsqrt_fusion, bf16[16,128,4096]{2,1,0:T(8,128)(2,1)} %bitcast.80, bf16[1,256,4096]{2,1,0:T(8,128)(2,1)} %param.15), kind=kOutput, calls=%fused_computation.18 | convolution fusion | flops 4297060352 | bytes 23109632 | tf_op jit(solution)/shard_map/dot_general | solution.py:61
  295.5 1.7 multiply_convert_fusion
  297.1 2.3 copy.69
  299.5 4.2 all-to-all-start
  303.9 75.8 %all-gather.14.cloned.1.call-done = bf16[1,1024,4096]{2,1,0:T(8,128)(2,1)} async-done(((bf16[1,256,4096]{2,1,0:T(8,128)(2,1)}), bf16[1,1024,4096]{2,1,0:T(8,128)(2,1)}) %all-gather.14.cloned.1.call-update) | async-done | bytes 8388624 | tf_op jit(solution)/shard_map/all_gather | solution.py:66
  379.8 10.2 %fusion.2 = bf16[512,4096]{1,0:T(8,128)(2,1)} fusion(bf16[1024,512]{1,0:T(8,128)(2,1)} %bitcast.23, bf16[1,1024,4096]{2,1,0:T(8,128)(2,1)} %all-gather.14.cloned.1.call-done), kind=kOutput, calls=%fused_computation.4 | convolution fusion | flops 4297064448 | bytes 13631488 | tf_op jit(solution)/shard_map/dot_general | solution.py:64
  390.1 2.7 convolution_bitcast_fusion
  392.7 2.6 copy.65
  397.9 2.1 fusion.7
  400.0 2.3 copy.70
  402.3 3.5 fusion.24
  405.8 11.9 %fusion.5 = bf16[1,256,4096]{2,1,0:T(8,128)(2,1)} fusion(bf16[256,2048]{0,1:T(8,128)(2,1)S(1)} %bitcast.90, bf16[2048,4096]{1,0:T(8,128)(2,1)} %all-gather.8.cloned.1.call-done), kind=kOutput, calls=%fused_computation.6 | convolution fusion | flops 4296015872 | bytes 19922944 | tf_op jit(solution)/shard_map/dot_general | solution.py:58
  417.8 56.0 %reduce-scatter.2.cloned.1.call-done = bf16[16,4096]{1,0:T(8,128)(2,1)} async-done(((bf16[512,4096]{1,0:T(8,128)(2,1)}), bf16[16,4096]{1,0:T(8,128)(2,1)}) %reduce-scatter.2.cloned.1.call-update) | async-done | bytes 131088 | tf_op jit(solution)/shard_map/reduce_scatter | solution.py:71
  473.7 1.6 convert_multiply_fusion
  475.3 113.5 %all-gather.12.cloned.1.call-done = f32[512,128,128]{2,1,0:T(8,128)} async-done(((f32[16,128,128]{2,1,0:T(8,128)}), f32[512,128,128]{2,1,0:T(8,128)}) %all-gather.12.cloned.1.call-update) | async-done | bytes 33554448 | tf_op jit(solution)/shard_map/all_gather | solution.py:16
  589.0 47.1 %while.23 = (s32[]{:T(128)}, f32[16,128,128]{2,1,0:T(8,128)S(1)}, s32[]{:T(128)}, f32[32,16,128,128]{3,2,1,0:T(8,128)}, s32[]{:T(128)}, /*index=5*/s32[]{:T(128)}, s32[]{:T(128)}, s32[]{:T(128)}) while((s32[]{:T(128)}, f32[16,128,128]{2,1,0:T(8,128)S(1)}, s32[]{:T(128)}, f32[32,16,128,128]{3,2,1,0:T(8,128)}, s32[]{:T(128)}, ...), condition=%wide.region_5.6_spmd, body=%wide.region_4.5_spmd.sunk | while | flops 262150 | bytes 3145871 | solution.py:23
  589.0 1.5 bitcast_add_fusion.8
  590.5 1.5 bitcast_add_fusion.8
  592.0 1.5 bitcast_add_fusion.8
  593.5 1.5 bitcast_add_fusion.8
  595.1 1.5 bitcast_add_fusion.8
  596.6 1.5 bitcast_add_fusion.8
  598.1 1.5 bitcast_add_fusion.8
  599.6 1.5 bitcast_add_fusion.8
  601.1 1.5 bitcast_add_fusion.8
  602.6 1.5 bitcast_add_fusion.8
  604.1 1.5 bitcast_add_fusion.8
  605.6 1.5 bitcast_add_fusion.8
  607.1 1.5 bitcast_add_fusion.8
  608.7 1.5 bitcast_add_fusion.8
  610.2 1.5 bitcast_add_fusion.8
  611.7 1.5 bitcast_add_fusion.8
  613.2 1.5 bitcast_add_fusion.8
  614.7 1.5 bitcast_add_fusion.8
  616.2 1.5 bitcast_add_fusion.8
  617.7 1.5 bitcast_add_fusion.8
  619.2 1.5 bitcast_add_fusion.8
  620.7 1.5 bitcast_add_fusion.8
  622.3 1.5 bitcast_add_fusion.8
  623.8 1.5 bitcast_add_fusion.8
  625.3 1.5 bitcast_add_fusion.8
  626.8 1.5 bitcast_add_fusion.8
  640.0 2.7 add_convert_fusion
  (61 shorter events, 23.6 us)
Async XLA Ops:
  7.2 120.8 %all-gather.10.cloned.1.call-start = ((), (), s32[]{:S(2)}) async-start(), calls=%async_computation.4 | async-start | bytes 34603008 | tf_op jit(solution)/shard_map/all_gather | solution.py:16
  7.2 2.5 copy-start.12
  8.8 1.0 copy-start.5
  9.7 1.7 copy-start.3
  11.4 271.4 %all-gather.8.cloned.1.call-start = ((), (), s32[]{:S(2)}) async-start(), calls=%async_computation.2 | async-start | bytes 20971520 | tf_op jit(solution)/shard_map/all_gather | solution.py:57
  12.2 2.3 copy-start.6
  12.2 367.6 %all-gather.14.cloned.1.call-start = ((), (), s32[]{:S(2)}) async-start(), calls=%async_computation.6 | async-start | bytes 10485760 | tf_op jit(solution)/shard_map/all_gather | solution.py:66
  14.4 113.6 %copy-start = (bf16[32,8,16,128]{3,2,1,0:T(8,128)(2,1)}, bf16[32,8,16,128]{3,2,1,0:T(8,128)(2,1)S(1)}, u32[]{:S(2)}) copy-start(bf16[32,8,16,128]{3,2,1,0:T(8,128)(2,1)S(1)} %copy.77) | copy-start | bytes 3145732
  15.2 1.3 copy-start.11
  128.0 154.8 %copy-start.13 = (f32[2048]{0:T(1024)S(1)}, f32[2048]{0:T(1024)}, u32[]{:S(2)}) copy-start(f32[2048]{0:T(1024)} %param.13) | copy-start | bytes 24580
  282.8 12.6 %copy-start.10 = (f32[256,16,128]{0,2,1:T(8,128)S(1)}, f32[256,16,128]{0,2,1:T(8,128)}, u32[]{:S(2)}) copy-start(f32[256,16,128]{0,2,1:T(8,128)} %get-tuple-element.128) | copy-start | bytes 6291460
  299.5 80.3 %all-to-all-start = ((bf16[256,4,512]{2,0,1:T(8,128)(2,1)}), bf16[256,4,512]{2,0,1:T(8,128)(2,1)}, u32[]{:S(2)}, u32[]{:S(2)}) async-start(bf16[256,4,512]{2,0,1:T(8,128)(2,1)} %copy.69), calls=%async_computation | async-start | bytes 2097152 | tf_op jit(solution)/shard_map/all_to_all | solution.py:60
  303.7 170.0 %reduce-scatter.2.cloned.1.call-start = ((), (), s32[]{:S(2)}) async-start(), calls=%async_computation.3 | async-start | bytes 4325376 | tf_op jit(solution)/shard_map/reduce_scatter | solution.py:71
  390.0 198.9 %all-gather.12.cloned.1.call-start = ((), (), s32[]{:S(2)}) async-start(), calls=%async_computation.5 | async-start | bytes 34603008 | tf_op jit(solution)/shard_map/all_gather | solution.py:16
  395.3 1.2 copy-start.4
  396.6 1.4 copy-start.8
  402.3 3.5 copy-start.2
  636.1 1.2 copy-start.1
  636.1 1.9 copy-start.9
  638.6 1.4 copy-start.7
Sparse Core Ops, SparseCore 0:
  11.6 116.3 all-gather.9
  129.6 153.2 all-gather.7
  284.5 95.2 all-gather.13
  390.1 83.5 reduce-scatter.1
  475.8 113.0 all-gather.11
where the time goes:
time: 652 us; the launch traced here: 651 us
  waiting for transfers between devices  507 us (78%)
  matrix products  57.5 us (9%)
  other arithmetic  49.5 us (8%)
  local copies, waits for them, and re-layouts  17.5 us (3%)
  between operations  14 us (2%)
    all_gather x2, waiting for transfers between devices, prefix(): gathered = lax.all_gather(part, axis)  223 us
    all_gather x1, waiting for transfers between devices, shards(): full_weight = lax.all_gather(out_weight, 'dp', axis=0, tiled=True)  151 us
    all_gather x1, waiting for transfers between devices, shards(): lax.all_gather(grad_rows, 'dp', axis=0, tiled=True)  75.8 us
    reduce_scatter x1, waiting for transfers between devices, shards(): lax.psum_scatter(weight_term.astype(jnp.bfloat16), 'ctx', scatter_dimensi...  56 us
    add x31, other arithmetic, add_terms(): return earlier + later_part  46.1 us
  transfers between devices with their start and end apart: 6, of which 5 were waited for; matrix products, arithmetic and copies ran while one was open for 8% of the time, Pallas kernels for 0%

commit v1 on v0

--- a/solution.py
+++ b/solution.py
@@ -54,7 +54,9 @@
     gain_heads = gain.reshape(head_count, HD)
     normed = (unit_out * gain_heads).astype(jnp.bfloat16).reshape(tok_rows, feat_width)
     grad_rows = grad_out.reshape(tok_rows, model_width)
-    full_weight = lax.all_gather(out_weight, "dp", axis=0, tiled=True)
+    full_weight = jnp.concatenate(
+        lax.all_to_all(jnp.stack([out_weight] * lax.axis_size("dp")), "dp", 0, 0), axis=0
+    )
     layer_rows = jnp.dot(normed, full_weight, preferred_element_type=jnp.float32)
     layer_out = layer_rows.astype(jnp.bfloat16).reshape(1, tok_rows, model_width)
     shared_cols = lax.all_to_all(normed, "dp", split_axis=1, concat_axis=0, tiled=True)

time: 652 us -> 584 us (0.90)
  waiting for transfers between devices: 507 us -> 423 us
  local copies, waits for them, and re-layouts: 17.5 us -> 24.9 us
  starting transfers between devices: 4.62 us -> 11.7 us
    all_gather x1 -> x0, waiting for transfers between devices: 151 us -> none  [shards(): full_weight = lax.all_gather(out_weight, 'dp', axis=0, tiled=True)]
    all_to_all x0 -> x1, waiting for transfers between devices: none -> 144 us  [shards(): lax.all_to_all(jnp.stack([out_weight] * lax.axis_size('dp')), 'dp', 0, 0)]
    all_gather x1, waiting for transfers between devices: 75.8 us -> 0.02 us  [shards(): lax.all_gather(grad_rows, 'dp', axis=0, tiled=True)]
    all_gather x2, waiting for transfers between devices: 223 us -> 209 us  [prefix(): gathered = lax.all_gather(part, axis)]
    all_to_all x1, waiting for transfers between devices: 0.01 us -> 11.3 us  [shards(): lax.all_to_all(normed, 'dp', split_axis=1, concat_axis=0, tiled=True)]
    another operation x2 -> x3, local copies, waits for them, and re-layouts: 0.19 us -> 7.65 us  [the longest x1 7.46 us: shards(): jnp.stack([out_weight] * lax.axis_size('dp'))]
    all_to_all x0 -> x1, starting transfers between devices: none -> 7.11 us  [shards(): lax.all_to_all(jnp.stack([out_weight] * lax.axis_size('dp')), 'dp', 0, 0)]
  transfers between devices with their start and end apart: 6 -> 6, of which waited for: 5 -> 5; matrix products, arithmetic and copies ran while one was open for 8% -> 10% of each run, Pallas kernels for 0% -> 0%
where the time goes in v1:
time: 584 us; the launch traced here: 582 us
  waiting for transfers between devices  423 us (72%)
  matrix products  57.6 us (10%)
  other arithmetic  49.5 us (8%)
  local copies, waits for them, and re-layouts  24.9 us (4%)
  between operations  14 us (2%)
  starting transfers between devices  11.7 us (2%)
    all_gather x2, waiting for transfers between devices, prefix(): gathered = lax.all_gather(part, axis)  209 us
    all_to_all x1, waiting for transfers between devices, shards(): lax.all_to_all(jnp.stack([out_weight] * lax.axis_size('dp')), 'dp', 0, 0)  144 us
    reduce_scatter x1, waiting for transfers between devices, shards(): lax.psum_scatter(weight_term.astype(jnp.bfloat16), 'ctx', scatter_dimensi...  58.2 us
    add x31, other arithmetic, add_terms(): return earlier + later_part  46.1 us
    dot_general x1, matrix products, shards(): lax.dot_general(grad_rows, full_weight, (((1,), (1,)), ((), ())), preferr...  12.6 us
    dot_general x1, matrix products, shards(): jnp.dot(normed, full_weight, preferred_element_type=jnp.float32)  12 us
  transfers between devices with their start and end apart: 6, of which 5 were waited for; matrix products, arithmetic and copies ran while one was open for 10% of the time, Pallas kernels for 0%

profile of v1, /device:TPU:0, one launch (start us, length us, event | category | flops | bytes accessed | tf_op | source)
XLA Modules:
  0.0 582.1 jit_solution(593718523930405532)
XLA Ops:
  7.2 1.5 copy.78
  11.5 7.5 %stack.2 = bf16[4,512,4096]{2,1,0:T(8,128)(2,1)} broadcast(bf16[512,4096]{1,0:T(8,128)(2,1)} %param.14), dimensions={1,2} | broadcast | bytes 20971520 | tf_op jit(solution)/shard_map/stack | solution.py:58
  19.0 7.1 %all-to-all-start = ((bf16[4,512,4096]{2,1,0:T(8,128)(2,1)}), bf16[4,512,4096]{2,1,0:T(8,128)(2,1)}, u32[]{:S(2)}, u32[]{:S(2)}) async-start(bf16[4,512,4096]{2,1,0:T(8,128)(2,1)} %stack.2), calls=%async_computation | async-start | bytes 33554432 | tf_op jit(solution)/shard_map/all_to_all | solution.py:58
  30.4 2.2 fusion.12
  32.6 95.4 %all-gather.7.cloned.1.call-done = f32[512,128,128]{2,1,0:T(8,128)} async-done(((f32[16,128,128]{2,1,0:T(8,128)}), f32[512,128,128]{2,1,0:T(8,128)}) %all-gather.7.cloned.1.call-update) | async-done | bytes 33554448 | tf_op jit(solution)/shard_map/all_gather | solution.py:16
  128.1 4.1 multiply_reduce_fusion.1
  132.2 144.1 %all-to-all-done = bf16[4,512,4096]{2,1,0:T(8,128)(2,1)} async-done(((bf16[4,512,4096]{2,1,0:T(8,128)(2,1)}), bf16[4,512,4096]{2,1,0:T(8,128)(2,1)}, u32[]{:S(2)}, u32[]{:S(2)}) %all-to-all-start) | async-done | bytes 16777248 | tf_op jit(solution)/shard_map/all_to_all | solution.py:58
  276.4 12.6 %multiply_reduce_fusion = (f32[256,16]{0,1:T(8,128)S(1)}, f32[256,16,128]{0,2,1:T(8,128)S(1)}) fusion(f32[256,16,128]{0,2,1:T(8,128)} %get-tuple-element.128, f32[16,128]{1,0:T(8,128)S(1)} %bitcast.102, f32[256,16]{0,1:T(8,128)S(1)} %add_rsqrt_fusion, bf16[16,128,4096]{2,1,0:T(8,128)(2,1)} %bitcast.11, bf16[1,256,4096]{2,1,0:T(8,128)(2,1)} %param.15), kind=kOutput, calls=%fused_computation.18 | convolution fusion | flops 4297060352 | bytes 23109632 | tf_op jit(solution)/shard_map/dot_general | solution.py:63
  289.0 1.7 multiply_convert_fusion
  290.7 2.3 copy.69
  293.0 4.2 all-to-all-start.1
  297.5 11.3 %all-to-all-done.1 = bf16[256,4,512]{2,0,1:T(8,128)(2,1)} async-done(((bf16[256,4,512]{2,0,1:T(8,128)(2,1)}), bf16[256,4,512]{2,0,1:T(8,128)(2,1)}, u32[]{:S(2)}, u32[]{:S(2)}) %all-to-all-start.1) | async-done | bytes 1048608 | tf_op jit(solution)/shard_map/all_to_all | solution.py:62
  308.8 10.4 %fusion.2 = bf16[512,4096]{1,0:T(8,128)(2,1)} fusion(bf16[1024,512]{1,0:T(8,128)(2,1)} %bitcast.24, bf16[1,1024,4096]{2,1,0:T(8,128)(2,1)} %all-gather.11.cloned.1.call-done), kind=kOutput, calls=%fused_computation.4 | convolution fusion | flops 4297064448 | bytes 13631488 | tf_op jit(solution)/shard_map/dot_general | solution.py:66
  319.2 2.7 convolution_bitcast_fusion
  321.9 2.5 copy.65
  327.0 2.1 fusion.7
  329.1 2.3 copy.70
  331.4 3.5 fusion.24
  334.9 12.0 %fusion.5 = bf16[1,256,4096]{2,1,0:T(8,128)(2,1)} fusion(bf16[256,2048]{0,1:T(8,128)(2,1)S(1)} %bitcast.90, bf16[2048,4096]{1,0:T(8,128)(2,1)} %bitcast.7), kind=kOutput, calls=%fused_computation.6 | convolution fusion | flops 4296015872 | bytes 19922944 | tf_op jit(solution)/shard_map/dot_general | solution.py:60
  346.9 58.2 %reduce-scatter.2.cloned.1.call-done = bf16[16,4096]{1,0:T(8,128)(2,1)} async-done(((bf16[512,4096]{1,0:T(8,128)(2,1)}), bf16[16,4096]{1,0:T(8,128)(2,1)}) %reduce-scatter.2.cloned.1.call-update) | async-done | bytes 131088 | tf_op jit(solution)/shard_map/reduce_scatter | solution.py:73
  405.1 1.6 convert_multiply_fusion
  406.7 113.6 %all-gather.9.cloned.1.call-done = f32[512,128,128]{2,1,0:T(8,128)} async-done(((f32[16,128,128]{2,1,0:T(8,128)}), f32[512,128,128]{2,1,0:T(8,128)}) %all-gather.9.cloned.1.call-update) | async-done | bytes 33554448 | tf_op jit(solution)/shard_map/all_gather | solution.py:16
  520.4 47.1 %while.23 = (s32[]{:T(128)}, f32[16,128,128]{2,1,0:T(8,128)S(1)}, s32[]{:T(128)}, f32[32,16,128,128]{3,2,1,0:T(8,128)}, s32[]{:T(128)}, /*index=5*/s32[]{:T(128)}, s32[]{:T(128)}, s32[]{:T(128)}) while((s32[]{:T(128)}, f32[16,128,128]{2,1,0:T(8,128)S(1)}, s32[]{:T(128)}, f32[32,16,128,128]{3,2,1,0:T(8,128)}, s32[]{:T(128)}, ...), condition=%wide.region_5.6_spmd, body=%wide.region_4.5_spmd.sunk | while | flops 262150 | bytes 3145871 | solution.py:23
  520.4 1.5 bitcast_add_fusion.8
  521.9 1.5 bitcast_add_fusion.8
  523.4 1.5 bitcast_add_fusion.8
  525.0 1.5 bitcast_add_fusion.8
  526.5 1.5 bitcast_add_fusion.8
  528.0 1.5 bitcast_add_fusion.8
  529.5 1.5 bitcast_add_fusion.8
  531.0 1.5 bitcast_add_fusion.8
  532.5 1.5 bitcast_add_fusion.8
  534.0 1.5 bitcast_add_fusion.8
  535.5 1.5 bitcast_add_fusion.8
  537.0 1.5 bitcast_add_fusion.8
  538.6 1.5 bitcast_add_fusion.8
  540.1 1.5 bitcast_add_fusion.8
  541.6 1.5 bitcast_add_fusion.8
  543.1 1.5 bitcast_add_fusion.8
  544.6 1.5 bitcast_add_fusion.8
  546.1 1.5 bitcast_add_fusion.8
  547.6 1.5 bitcast_add_fusion.8
  549.1 1.5 bitcast_add_fusion.8
  550.6 1.5 bitcast_add_fusion.8
  552.2 1.5 bitcast_add_fusion.8
  553.7 1.5 bitcast_add_fusion.8
  558.2 1.5 bitcast_add_fusion.8
  571.4 2.7 add_convert_fusion
  (61 shorter events, 25.9 us)
Async XLA Ops:
  7.2 120.8 %all-gather.7.cloned.1.call-start = ((), (), s32[]{:S(2)}) async-start(), calls=%async_computation.4 | async-start | bytes 34603008 | tf_op jit(solution)/shard_map/all_gather | solution.py:16
  7.2 2.6 copy-start.12
  8.8 1.0 copy-start.5
  9.8 1.7 copy-start.3
  19.0 257.4 %all-to-all-start = ((bf16[4,512,4096]{2,1,0:T(8,128)(2,1)}), bf16[4,512,4096]{2,1,0:T(8,128)(2,1)}, u32[]{:S(2)}, u32[]{:S(2)}) async-start(bf16[4,512,4096]{2,1,0:T(8,128)(2,1)} %stack.2), calls=%async_computation | async-start | bytes 33554432 | tf_op jit(solution)/shard_map/all_to_all | solution.py:58
  26.1 2.3 copy-start.6
  26.1 271.4 %all-gather.11.cloned.1.call-start = ((), (), s32[]{:S(2)}) async-start(), calls=%async_computation.6 | async-start | bytes 10485760 | tf_op jit(solution)/shard_map/all_gather | solution.py:68
  28.3 99.8 %copy-start = (bf16[32,8,16,128]{3,2,1,0:T(8,128)(2,1)}, bf16[32,8,16,128]{3,2,1,0:T(8,128)(2,1)S(1)}, u32[]{:S(2)}) copy-start(bf16[32,8,16,128]{3,2,1,0:T(8,128)(2,1)S(1)} %copy.77) | copy-start | bytes 3145732
  29.1 1.3 copy-start.11
  128.1 148.3 %copy-start.13 = (f32[2048]{0:T(1024)S(1)}, f32[2048]{0:T(1024)}, u32[]{:S(2)}) copy-start(f32[2048]{0:T(1024)} %param.13) | copy-start | bytes 24580
  276.4 12.6 %copy-start.10 = (f32[256,16,128]{0,2,1:T(8,128)S(1)}, f32[256,16,128]{0,2,1:T(8,128)}, u32[]{:S(2)}) copy-start(f32[256,16,128]{0,2,1:T(8,128)} %get-tuple-element.128) | copy-start | bytes 6291460
  293.0 15.8 %all-to-all-start.1 = ((bf16[256,4,512]{2,0,1:T(8,128)(2,1)}), bf16[256,4,512]{2,0,1:T(8,128)(2,1)}, u32[]{:S(2)}, u32[]{:S(2)}) async-start(bf16[256,4,512]{2,0,1:T(8,128)(2,1)} %copy.69), calls=%async_computation.1 | async-start | bytes 2097152 | tf_op jit(solution)/shard_map/all_to_all | solution.py:62
  297.2 107.9 %reduce-scatter.2.cloned.1.call-start = ((), (), s32[]{:S(2)}) async-start(), calls=%async_computation.3 | async-start | bytes 4325376 | tf_op jit(solution)/shard_map/reduce_scatter | solution.py:73
  319.1 201.1 %all-gather.9.cloned.1.call-start = ((), (), s32[]{:S(2)}) async-start(), calls=%async_computation.5 | async-start | bytes 34603008 | tf_op jit(solution)/shard_map/all_gather | solution.py:16
  324.4 1.2 copy-start.4
  325.6 1.4 copy-start.8
  331.4 3.5 copy-start.2
  567.5 1.2 copy-start.1
  567.5 1.9 copy-start.9
  570.0 1.4 copy-start.7
Sparse Core Ops, SparseCore 0:
  11.6 116.3 all-gather.6
  129.6 147.7 all-gather.10
  319.3 85.7 reduce-scatter.1
  407.2 113.0 all-gather.8
